TPU v7x, 128 devices: a whole 4x4x4 slice. The times are simulated.
128 devices in a mesh: replica: 16 (over x_lo, z, core), shard: 8 (over y, x_hi).
Axes of the slice: x: 4 (x_hi: 2, x_lo: 2; x = x_hi * 2 + x_lo), y: 4, z: 4, core: 2. Of those that a mesh axis runs over, the one named last changes fastest.
Arguments:
- weights: bfloat16 [16, 2560, 7168], P('replica', None, 'shard'), may hold values from -60 to 60, as said below
- inputs: bfloat16 [8192, 2560], P('replica'), may hold values from -0.125 to 0.125
- targets: bfloat16 [8192, 7168], P('replica', 'shard'), may hold values from -6 to 6
- factors: float32 [3, 7168, 16], P(None, 'shard'), may hold values from -6 to 6
Outputs:
- mixed: bfloat16 [16, 2560, 7168], P('replica', None, 'shard')
Inputs may be any that keep to these rules, and one draw needn't show every extreme that they name: `weights`: independent entries for every replica.
All inputs are finite; a program needn't handle non-finite values.
Results may differ from a plain program's by a relative error of at most 0.0075.
Values may be sent and summed in bfloat16 or wider, within the bound.
A program may use at most 64 MiB of HBM per device.

v0:
```python
import jax
import jax.numpy as jnp
from jax import lax
from jax.sharding import PartitionSpec as P

ROUNDS = 3
RANK = 16
DISTANCES = (1, 2, 4)
HIGH = lax.Precision.HIGHEST
F32, BF16 = (jnp.float32, jnp.bfloat16)
NT = (((1,), (1,)), ((), ()))
NN = (((1,), (0,)), ((), ()))
TN = (((0,), (0,)), ((), ()))


def mm(a, b, dims):
    return lax.dot_general(a.astype(BF16), b.astype(BF16), dims, preferred_element_type=F32)


def passed_along(value, axis, steps):
    count = lax.axis_size(axis)
    pairs = [(source, (source + steps) % count) for source in range(count)]
    return lax.ppermute(value, axis, pairs)


def orthonormal(diff):
    gram = lax.dot_general(diff, diff, NT, precision=HIGH, preferred_element_type=F32)
    lower = jnp.linalg.cholesky(gram)
    solved = lax.linalg.triangular_solve(lower, diff, left_side=True, lower=True)
    return solved.astype(BF16)


def per_device(weights, x, targets, factors):
    weight = weights[0]
    qb = factors.astype(BF16).transpose(0, 2, 1).reshape(ROUNDS * RANK, -1)
    partial = jnp.concatenate([mm(qb, weight, NT), mm(qb, targets, NT)], axis=1)
    total = lax.psum(partial, "shard")
    depth = weight.shape[0]
    shared, goal = (total[:, :depth], total[:, depth:])
    first = mm(x, weight, NN) - targets.astype(F32)
    gram_x = mm(x, x, NT)
    sums = [first]
    for _ in range(ROUNDS - 1):
        sums.append(first + sums[-1] - 0.3 * mm(gram_x, sums[-1], NN))
    grown = weight.astype(F32) - 0.3 * mm(x, sums[-1], TN)
    bases, rights = ([], [])
    for step in range(ROUNDS):
        dist = DISTANCES[step]
        shared = shared - 0.3 * mm(mm(shared, x, NT) - goal, x, NN)
        left = shared[:RANK]
        basis = orthonormal(left - passed_along(left, "replica", dist))
        shared, goal = (shared[RANK:], goal[RANK:])
        if step < ROUNDS - 1:
            inner = mm(shared, basis, NT)
            inner = inner - passed_along(inner, "replica", dist)
            shared = shared - 0.5 * mm(inner, basis, NN)
        inside = mm(basis, x, NT)
        right = mm(basis, weight, NN) - 0.3 * mm(inside, sums[step], NN)
        for old, old_right in zip(bases, rights):
            right = right - 0.5 * mm(mm(basis, old, NT), old_right, NN)
        rights.append(right - passed_along(right, "replica", dist))
        bases.append(basis)
        if step < ROUNDS - 1:
            bases = [old.astype(F32) - 0.3 * mm(mm(old, x, NT), x, NN) for old in bases]
    low_rank = mm(jnp.concatenate([b.astype(F32) for b in bases]), jnp.concatenate(rights), TN)
    return (grown - 0.5 * low_rank).astype(BF16)[None]


def solution(mesh):
    in_specs = (
        P("replica", None, "shard"),
        P("replica", None),
        P("replica", "shard"),
        P(None, "shard", None),
    )
    out_specs = P("replica", None, "shard")
    return jax.shard_map(
        per_device, mesh=mesh, in_specs=in_specs, out_specs=out_specs, check_vma=False
    )
```

profile of v0, /device:TPU:0, one launch (start us, length us, event | category | flops | bytes accessed | tf_op | source)
XLA Modules:
  0.0 217.2 jit_solution(6847564169925928657)
XLA Ops:
  7.6 3.9 %fusion.9 = f32[48,2560]{1,0:T(8,128)S(1)} fusion(bf16[48,896]{1,0:T(8,128)(2,1)S(1)} %bitcast.108, bf16[1,2560,896]{2,1,0:T(8,128)(2,1)} %param.7), kind=kOutput, calls=%fused_computation.10 | convolution fusion | flops 220200960 | bytes 5165056 | tf_op jit(solution)/shard_map/dot_general | solution.py:17
  12.8 5.2 %convert_subtract_fusion = f32[512,896]{1,0:T(8,128)S(1)} fusion(bf16[512,896]{1,0:T(8,128)(2,1)S(1)} %copy-done.8, bf16[512,2560]{1,0:T(8,128)(2,1)S(1)} %copy-done, bf16[1,2560,896]{2,1,0:T(8,128)(2,1)} %param.7), kind=kOutput, calls=%fused_computation.34 | convolution fusion | flops 2349727744 | bytes 9961472 | tf_op jit(solution)/shard_map/dot_general | solution.py:17
  20.4 2.0 multiply_subtract_fusion
  22.3 80.1 %all-reduce.2.cloned.1.call-done = f32[48,3072]{1,0:T(8,128)} async-done(((f32[48,3072]{1,0:T(8,128)}), f32[48,3072]{1,0:T(8,128)}) %all-reduce.2.cloned.1.call-update) | async-done | bytes 589840 | tf_op jit(solution)/shard_map/psum | solution.py:37
  102.4 2.6 %fusion.13 = f32[48,2560]{1,0:T(8,128)S(1)} fusion(bf16[512,2560]{1,0:T(8,128)(2,1)S(1)} %copy-done, f32[48,3072]{1,0:T(8,128)} %all-reduce.2.cloned.1.call-done), kind=kOutput, calls=%fused_computation.15 | convolution fusion | flops 252076032 | bytes 6815744 | tf_op jit(solution)/shard_map/dot_general | solution.py:17
  105.2 4.4 %subtract_convert_fusion = bf16[512,896]{1,0:T(8,128)(2,1)} fusion(f32[512,896]{1,0:T(8,128)} %copy-done.2, f32[512,896]{1,0:T(8,128)} %multiply_subtract_fusion, bf16[512,512]{1,0:T(8,128)(2,1)} %copy-done.11), kind=kOutput, calls=%fused_computation.32 | convolution fusion | flops 472055808 | bytes 5111808 | tf_op jit(solution)/shard_map/dot_general | solution.py:17
  109.6 2.4 %collective-permute-done = f32[16,2560]{1,0:T(8,128)S(1)} collective-permute-done((f32[16,2560]{1,0:T(8,128)S(1)}, f32[16,2560]{1,0:T(8,128)S(1)}, u32[]{:S(2)}, u32[]{:S(2)}) %collective-permute-start) | collective-permute-done | bytes 163872 | tf_op jit(solution)/shard_map/ppermute | solution.py:23
  117.0 3.0 %fusion.7 = f32[16,896]{1,0:T(8,128)S(1)} fusion(bf16[16,2560]{1,0:T(8,128)(2,1)S(1)} %convolution_convert_fusion.2, bf16[1,2560,896]{2,1,0:T(8,128)(2,1)} %param.7), kind=kOutput, calls=%fused_computation.8 | convolution fusion | flops 73400320 | bytes 4726784 | tf_op jit(solution)/shard_map/dot_general | solution.py:17
  122.5 1.8 fusion.19
  127.0 2.5 %fusion.14 = f32[32,2560]{1,0:T(8,128)S(1)} fusion(f32[32,2560]{1,0:T(8,128)} %fusion.15, bf16[512,2560]{1,0:T(8,128)(2,1)S(1)} %copy-done, f32[48,3072]{1,0:T(8,128)} %all-reduce.2.cloned.1.call-done), kind=kOutput, calls=%fused_computation.17 | convolution fusion | flops 168050688 | bytes 6291456 | tf_op jit(solution)/shard_map/dot_general | solution.py:17
  130.5 6.5 %collective-permute-done.2 = f32[16,2560]{1,0:T(8,128)S(1)} collective-permute-done((f32[16,2560]{1,0:T(8,128)S(1)}, f32[16,2560]{1,0:T(8,128)S(1)}, u32[]{:S(2)}, u32[]{:S(2)}) %collective-permute-start.2) | collective-permute-done | bytes 163872 | tf_op jit(solution)/shard_map/ppermute | solution.py:23
  141.8 3.0 %fusion.5 = f32[16,896]{1,0:T(8,128)S(1)} fusion(bf16[16,2560]{1,0:T(8,128)(2,1)S(1)} %convolution_convert_fusion.1, bf16[1,2560,896]{2,1,0:T(8,128)(2,1)} %param.7), kind=kOutput, calls=%fused_computation.6 | convolution fusion | flops 73400320 | bytes 4726784 | tf_op jit(solution)/shard_map/dot_general | solution.py:17
  147.8 5.4 %collective-permute-done.3 = f32[16,16]{1,0:T(8,128)S(1)} collective-permute-done((f32[16,16]{1,0:T(8,128)S(1)}, f32[16,16]{1,0:T(8,128)S(1)}, u32[]{:S(2)}, u32[]{:S(2)}) %collective-permute-start.3) | collective-permute-done | bytes 1056 | tf_op jit(solution)/shard_map/ppermute | solution.py:23
  153.3 2.0 fusion.16
  155.9 7.1 %collective-permute-done.4 = f32[16,2560]{1,0:T(8,128)S(1)} collective-permute-done((f32[16,2560]{1,0:T(8,128)S(1)}, f32[16,2560]{1,0:T(8,128)S(1)}, u32[]{:S(2)}, u32[]{:S(2)}) %collective-permute-start.4) | collective-permute-done | bytes 163872 | tf_op jit(solution)/shard_map/ppermute | solution.py:23
  164.7 2.1 cholesky.81
  171.4 3.6 %fusion.3 = f32[16,896]{1,0:T(8,128)} fusion(bf16[16,2560]{1,0:T(8,128)(2,1)S(1)} %convolution_convert_fusion, bf16[1,2560,896]{2,1,0:T(8,128)(2,1)} %param.7), kind=kOutput, calls=%fused_computation.4 | convolution fusion | flops 73400320 | bytes 4726784 | tf_op jit(solution)/shard_map/dot_general | solution.py:17
  175.0 2.5 %fusion.25 = f32[16,896]{1,0:T(8,128)} fusion(f32[16,896]{1,0:T(8,128)} %fusion.3, bf16[512,896]{1,0:T(8,128)(2,1)S(1)} %copy-done.4, bf16[16,2560]{1,0:T(8,128)(2,1)} %copy-done.5, bf16[512,2560]{1,0:T(8,128)(2,1)S(1)} %copy-done), kind=kOutput, calls=%fused_computation.44 | convolution fusion | flops 56659968 | bytes 3735552 | tf_op jit(solution)/shard_map/dot_general | solution.py:17
  177.6 1.8 fusion.24
  179.4 1.8 fusion.23
  181.3 6.1 %fusion.71 = f32[896,2560]{1,0:T(8,128)} fusion(bf16[512,896]{1,0:T(8,128)(2,1)S(1)} %copy-done.4, bf16[512,2560]{1,0:T(8,128)(2,1)S(1)} %copy-done), kind=kOutput, calls=%fused_computation.122 | convolution fusion | flops 2348810240 | bytes 12713984 | tf_op jit(solution)/shard_map/dot_general | solution.py:17
  187.4 7.3 %copy.5 = bf16[1,2560,896]{1,2,0:T(8,128)(2,1)} copy(bf16[1,2560,896]{2,1,0:T(8,128)(2,1)} %param.7) | data formatting | bytes 9175040 | tf_op args[0]
  195.6 7.5 %fusion.2 = bf16[1,2560,896]{1,2,0:T(8,128)(2,1)} fusion(f32[896,2560]{1,0:T(8,128)} %fusion.71, bf16[1,2560,896]{1,2,0:T(8,128)(2,1)} %copy.5, bf16[16,2560]{1,0:T(8,128)(2,1)S(1)} %copy-done.6, bf16[16,2560]{1,0:T(8,128)(2,1)S(1)} %copy-done.9, bf16[16,2560]{1,0:T(8,128)(2,1)S(1)} %copy-done.10, bf16[16,896]{1,0:T(8,128)(2,1)S(1)} %subtract_convert_fusion.2, ...), kind=kOutput, calls=%fused_computation.3 | convolution fusion | flops 234958848 | bytes 18681856 | tf_op jit(solution)/shard_map/dot_general | solution.py:17
  203.2 7.2 %copy.10 = bf16[1,2560,896]{2,1,0:T(8,128)(2,1)} copy(bf16[1,2560,896]{1,2,0:T(8,128)(2,1)} %fusion.2) | data formatting | bytes 9175040 | tf_op jit(solution)/shard_map/broadcast_in_dim | solution.py:66
  (93 shorter events, 31.4 us)
Async XLA Ops:
  6.5 6.3 %copy-start = (bf16[512,2560]{1,0:T(8,128)(2,1)S(1)}, bf16[512,2560]{1,0:T(8,128)(2,1)}, u32[]{:S(2)}) copy-start(bf16[512,2560]{1,0:T(8,128)(2,1)} %param.8) | copy-start | bytes 7864324
  6.5 95.9 %all-reduce.2.cloned.1.call-start = ((), (), s32[]{:S(2)}) async-start(), calls=%async_computation | async-start | bytes 1179648 | tf_op jit(solution)/shard_map/psum | solution.py:37
  7.6 3.9 %copy-start.8 = (bf16[512,896]{1,0:T(8,128)(2,1)S(1)}, bf16[512,896]{1,0:T(8,128)(2,1)}, u32[]{:S(2)}) copy-start(bf16[512,896]{1,0:T(8,128)(2,1)} %param.9) | copy-start | bytes 2752516
  18.0 1.6 copy-start.2
  19.6 0.8 copy-start.11
  105.1 6.9 %collective-permute-start = (f32[16,2560]{1,0:T(8,128)S(1)}, f32[16,2560]{1,0:T(8,128)S(1)}, u32[]{:S(2)}, u32[]{:S(2)}) collective-permute-start(f32[16,2560]{1,0:T(8,128)S(1)} %slice.42), channel_id=1, source_target_pairs={{0,8},{8,16},{16,24},{24,32},{32,40},{40,48},{48,56},{56,64},{64,7... | collective-permute-start | bytes 491528 | tf_op jit(solution)/shard_map/ppermute | solution.py:23
  120.0 1.5 copy-start.3
  120.8 5.2 %collective-permute-start.1 = (f32[32,16]{0,1:T(8,128)S(1)}, f32[32,16]{0,1:T(8,128)S(1)}, u32[]{:S(2)}, u32[]{:S(2)}) collective-permute-start(f32[32,16]{0,1:T(8,128)S(1)} %fusion.40), channel_id=1, source_target_pairs={{0,8},{8,16},{16,24},{24,32},{32,40},{40,48},{48,56},{56,64},{64,7... | collective-permute-start | bytes 6152 | tf_op jit(solution)/shard_map/ppermute | solution.py:23
  122.4 7.2 %collective-permute-start.5 = (f32[16,896]{1,0:T(8,128)}, f32[16,896]{1,0:T(8,128)}, u32[]{:S(2)}, u32[]{:S(2)}) collective-permute-start(f32[16,896]{1,0:T(8,128)} %fusion.28), channel_id=1, source_target_pairs={{0,8},{8,16},{16,24},{24,32},{32,40},{40,48},{48,56},{56,64},{64,7... | collective-permute-start | bytes 172040 | tf_op jit(solution)/shard_map/ppermute | solution.py:23
  129.5 7.5 %collective-permute-start.2 = (f32[16,2560]{1,0:T(8,128)S(1)}, f32[16,2560]{1,0:T(8,128)S(1)}, u32[]{:S(2)}, u32[]{:S(2)}) collective-permute-start(f32[16,2560]{1,0:T(8,128)S(1)} %slice.45), channel_id=1, source_target_pairs={{0,16},{8,24},{16,32},{24,40},{32,48},{40,56},{48,64},{56,72},{64,... | collective-permute-start | bytes 491528 | tf_op jit(solution)/shard_map/ppermute | solution.py:23
  130.5 16.9 %copy-start.12 = (bf16[16,896]{1,0:T(8,128)(2,1)}, bf16[16,896]{1,0:T(8,128)(2,1)S(1)}, u32[]{:S(2)}) copy-start(bf16[16,896]{1,0:T(8,128)(2,1)S(1)} %subtract_convert_fusion.4) | copy-start | bytes 86020
  144.9 2.1 copy-start.1
  147.1 6.0 %collective-permute-start.3 = (f32[16,16]{1,0:T(8,128)S(1)}, f32[16,16]{1,0:T(8,128)S(1)}, u32[]{:S(2)}, u32[]{:S(2)}) collective-permute-start(f32[16,16]{1,0:T(8,128)S(1)} %fusion.54), channel_id=1, source_target_pairs={{0,16},{8,24},{16,32},{24,40},{32,48},{40,56},{48,64},{56,72},{64,... | collective-permute-start | bytes 3080 | tf_op jit(solution)/shard_map/ppermute | solution.py:23
  147.7 7.6 %collective-permute-start.6 = (f32[16,896]{1,0:T(8,128)S(1)}, f32[16,896]{1,0:T(8,128)S(1)}, u32[]{:S(2)}, u32[]{:S(2)}) collective-permute-start(f32[16,896]{1,0:T(8,128)S(1)} %fusion.26), channel_id=1, source_target_pairs={{0,16},{8,24},{16,32},{24,40},{32,48},{40,56},{48,64},{56,72},{64,... | collective-permute-start | bytes 172040 | tf_op jit(solution)/shard_map/ppermute | solution.py:23
  155.3 7.7 %collective-permute-start.4 = (f32[16,2560]{1,0:T(8,128)S(1)}, f32[16,2560]{1,0:T(8,128)S(1)}, u32[]{:S(2)}, u32[]{:S(2)}) collective-permute-start(f32[16,2560]{1,0:T(8,128)S(1)} %fusion.16), channel_id=1, source_target_pairs={{0,32},{8,40},{16,48},{24,56},{32,64},{40,72},{48,80},{56,88},{64,... | collective-permute-start | bytes 491528 | tf_op jit(solution)/shard_map/ppermute | solution.py:23
  163.0 0.7 copy-start.7
  163.7 11.4 %copy-start.4 = (bf16[512,896]{1,0:T(8,128)(2,1)S(1)}, bf16[512,896]{1,0:T(8,128)(2,1)}, u32[]{:S(2)}) copy-start(bf16[512,896]{1,0:T(8,128)(2,1)} %subtract_convert_fusion) | copy-start | bytes 2752516
  181.3 13.5 %collective-permute-start.7 = (f32[16,896]{1,0:T(8,128)}, f32[16,896]{1,0:T(8,128)}, u32[]{:S(2)}, u32[]{:S(2)}) collective-permute-start(f32[16,896]{1,0:T(8,128)} %fusion.23), channel_id=1, source_target_pairs={{0,32},{8,40},{16,48},{24,56},{32,64},{40,72},{48,80},{56,88},{64,... | collective-permute-start | bytes 172040 | tf_op jit(solution)/shard_map/ppermute | solution.py:23
  187.4 7.4 %copy-start.15 = (f32[16,896]{1,0:T(8,128)S(1)}, f32[16,896]{1,0:T(8,128)}, u32[]{:S(2)}) copy-start(f32[16,896]{1,0:T(8,128)} %fusion.23) | copy-start | bytes 172036
  187.4 8.2 %copy-start.6 = (bf16[16,2560]{1,0:T(8,128)(2,1)S(1)}, bf16[16,2560]{1,0:T(8,128)(2,1)}, u32[]{:S(2)}) copy-start(bf16[16,2560]{1,0:T(8,128)(2,1)} %copy-done.5) | copy-start | bytes 245764
  187.4 8.2 %copy-start.9 = (bf16[16,2560]{1,0:T(8,128)(2,1)S(1)}, bf16[16,2560]{1,0:T(8,128)(2,1)}, u32[]{:S(2)}) copy-start(bf16[16,2560]{1,0:T(8,128)(2,1)} %subtract_convert_fusion.1) | copy-start | bytes 245764
  187.4 8.2 %copy-start.10 = (bf16[16,2560]{1,0:T(8,128)(2,1)S(1)}, bf16[16,2560]{1,0:T(8,128)(2,1)}, u32[]{:S(2)}) copy-start(bf16[16,2560]{1,0:T(8,128)(2,1)} %fusion.19) | copy-start | bytes 245764
  187.4 8.2 %copy-start.13 = (bf16[16,896]{1,0:T(8,128)(2,1)S(1)}, bf16[16,896]{1,0:T(8,128)(2,1)}, u32[]{:S(2)}) copy-start(bf16[16,896]{1,0:T(8,128)(2,1)} %copy-done.12) | copy-start | bytes 86020
  187.4 8.2 %copy-start.14 = (bf16[16,896]{1,0:T(8,128)(2,1)S(1)}, bf16[16,896]{1,0:T(8,128)(2,1)}, u32[]{:S(2)}) copy-start(bf16[16,896]{1,0:T(8,128)(2,1)} %subtract_convert_fusion.3) | copy-start | bytes 86020
  (1 other events, 0.6 us)
Sparse Core Ops, SparseCore 0:
  12.9 89.4 all-reduce.1
where the time goes:
time: 218 us; the launch traced here: 217 us
  waiting for transfers between devices  103 us (47%)
  matrix products  64.7 us (30%)
  other arithmetic  17.9 us (8%)
  local copies, waits for them, and re-layouts  17.1 us (8%)
  between operations  13.7 us (6%)
    psum x1, waiting for transfers between devices, per_device(): total = lax.psum(partial, 'shard')  80.1 us
    dot_general x29, matrix products, mm(): lax.dot_general(a.astype(BF16), b.astype(BF16), dims, preferred_element_t...  61.9 us
    ppermute x8, waiting for transfers between devices, passed_along(): return lax.ppermute(value, axis, pairs)  23.2 us
    unnamed x33, local copies, waits for them, and re-layouts  9.72 us
    another operation x9, other arithmetic, orthonormal(): lower = jnp.linalg.cholesky(gram)  7.34 us
    broadcast_in_dim x1, local copies, waits for them, and re-layouts, per_device(): return (grown - 0.5 * low_rank).astype(BF16)[None]  7.17 us
    another operation x6, other arithmetic, orthonormal(): lax.linalg.triangular_solve(lower, diff, left_side=True, lower=True)  5.65 us
  transfers between devices with their start and end apart: 9, of which 6 were waited for; matrix products, arithmetic and copies ran while one was open for 17% of the time, Pallas kernels for 0%

commit v1 on v0

--- a/solution.py
+++ b/solution.py
@@ -34,7 +34,7 @@
     weight = weights[0]
     qb = factors.astype(BF16).transpose(0, 2, 1).reshape(ROUNDS * RANK, -1)
     partial = jnp.concatenate([mm(qb, weight, NT), mm(qb, targets, NT)], axis=1)
-    total = lax.psum(partial, "shard")
+    total = jnp.sum(lax.all_gather(partial, "shard"), axis=0)
     depth = weight.shape[0]
     shared, goal = (total[:, :depth], total[:, depth:])
     first = mm(x, weight, NN) - targets.astype(F32)

time: 218 us -> 210 us (0.963)
  waiting for transfers between devices: 103 us -> 92.5 us
  other arithmetic: 17.9 us -> 21.1 us
  matrix products: 64.7 us -> 62.4 us
    psum x1 -> x0, waiting for transfers between devices: 80.1 us -> none  [per_device(): total = lax.psum(partial, 'shard')]
    all_gather x0 -> x1, waiting for transfers between devices: none -> 69.3 us  [per_device(): total = jnp.sum(lax.all_gather(partial, 'shard'), axis=0)]
    reduce_sum x0 -> x1, other arithmetic: none -> 3.47 us  [per_device(): total = jnp.sum(lax.all_gather(partial, 'shard'), axis=0)]
    dot_general x29, matrix products: 61.9 us -> 59.6 us  [mm(): lax.dot_general(a.astype(BF16), b.astype(BF16), dims, preferred_element_t...]
    unnamed x33 -> x39, local copies, waits for them, and re-layouts: 9.72 us -> 11.1 us
where the time goes in v1:
time: 210 us; the launch traced here: 209 us
  waiting for transfers between devices  92.5 us (44%)
  matrix products  62.4 us (30%)
  other arithmetic  21.1 us (10%)
  local copies, waits for them, and re-layouts  18.5 us (9%)
  between operations  13.7 us (7%)
    all_gather x1, waiting for transfers between devices, per_device(): total = jnp.sum(lax.all_gather(partial, 'shard'), axis=0)  69.3 us
    dot_general x29, matrix products, mm(): lax.dot_general(a.astype(BF16), b.astype(BF16), dims, preferred_element_t...  59.6 us
    ppermute x8, waiting for transfers between devices, passed_along(): return lax.ppermute(value, axis, pairs)  23.2 us
    unnamed x39, local copies, waits for them, and re-layouts  11.1 us
    another operation x9, other arithmetic, orthonormal(): lower = jnp.linalg.cholesky(gram)  7.17 us
    broadcast_in_dim x1, local copies, waits for them, and re-layouts, per_device(): return (grown - 0.5 * low_rank).astype(BF16)[None]  7.17 us
    another operation x6, other arithmetic, orthonormal(): lax.linalg.triangular_solve(lower, diff, left_side=True, lower=True)  5.47 us
  transfers between devices with their start and end apart: 9, of which 6 were waited for; matrix products, arithmetic and copies ran while one was open for 17% of the time, Pallas kernels for 0%

profile of v1, /device:TPU:0, one launch (start us, length us, event | category | flops | bytes accessed | tf_op | source)
XLA Modules:
  0.0 208.8 jit_solution(16968518541723266101)
XLA Ops:
  7.6 3.9 %fusion.9 = f32[48,2560]{1,0:T(8,128)S(1)} fusion(bf16[48,896]{1,0:T(8,128)(2,1)S(1)} %bitcast.112, bf16[1,2560,896]{2,1,0:T(8,128)(2,1)} %param.7), kind=kOutput, calls=%fused_computation.10 | convolution fusion | flops 220200960 | bytes 5165056 | tf_op jit(solution)/shard_map/dot_general | solution.py:17
  15.4 2.9 %convert_subtract_fusion = f32[512,896]{1,0:T(8,128)S(1)} fusion(bf16[512,896]{1,0:T(8,128)(2,1)S(1)} %copy-done.9, bf16[512,2560]{1,0:T(8,128)(2,1)S(1)} %copy-done, bf16[1,2560,896]{2,1,0:T(8,128)(2,1)S(1)} %bitcast.110), kind=kOutput, calls=%fused_computation.34 | convolution fusion | flops 2349727744 | bytes 9961472 | tf_op jit(solution)/shard_map/dot_general | solution.py:17
  19.5 2.0 multiply_subtract_fusion
  21.5 69.3 %all-gather.3.cloned.1.call-done = f32[384,3072]{1,0:T(8,128)} async-done(((f32[48,3072]{1,0:T(8,128)}), f32[384,3072]{1,0:T(8,128)}) %all-gather.3.cloned.1.call-update) | async-done | bytes 4718608 | tf_op jit(solution)/shard_map/all_gather | solution.py:37
  90.8 3.5 %reduce_sum.9 = f32[48,3072]{1,0:T(8,128)} reduce(f32[8,48,3072]{2,1,0:T(8,128)} %bitcast.111, f32[]{:T(128)} %constant.41.clone.1), dimensions={0}, to_apply=%region_0.0 | reduce | flops 1032192 | bytes 5308420 | tf_op jit(solution)/shard_map/reduce_sum | solution.py:37
  94.3 2.7 %fusion.13 = f32[48,2560]{1,0:T(8,128)S(1)} fusion(bf16[512,2560]{1,0:T(8,128)(2,1)S(1)} %copy-done, f32[48,3072]{1,0:T(8,128)} %reduce_sum.9), kind=kOutput, calls=%fused_computation.15 | convolution fusion | flops 252076032 | bytes 6815744 | tf_op jit(solution)/shard_map/dot_general | solution.py:17
  97.1 4.4 %subtract_convert_fusion = bf16[512,896]{1,0:T(8,128)(2,1)} fusion(f32[512,896]{1,0:T(8,128)} %copy-done.2, f32[512,896]{1,0:T(8,128)} %multiply_subtract_fusion, bf16[512,512]{1,0:T(8,128)(2,1)} %copy-done.12), kind=kOutput, calls=%fused_computation.32 | convolution fusion | flops 472055808 | bytes 5111808 | tf_op jit(solution)/shard_map/dot_general | solution.py:17
  101.5 2.4 %collective-permute-done = f32[16,2560]{1,0:T(8,128)S(1)} collective-permute-done((f32[16,2560]{1,0:T(8,128)S(1)}, f32[16,2560]{1,0:T(8,128)S(1)}, u32[]{:S(2)}, u32[]{:S(2)}) %collective-permute-start) | collective-permute-done | bytes 163872 | tf_op jit(solution)/shard_map/ppermute | solution.py:23
  108.8 3.0 %fusion.7 = f32[16,896]{1,0:T(8,128)S(1)} fusion(bf16[16,2560]{1,0:T(8,128)(2,1)S(1)} %convolution_convert_fusion.2, bf16[1,2560,896]{2,1,0:T(8,128)(2,1)} %param.7), kind=kOutput, calls=%fused_computation.8 | convolution fusion | flops 73400320 | bytes 4726784 | tf_op jit(solution)/shard_map/dot_general | solution.py:17
  118.8 2.5 %fusion.14 = f32[32,2560]{1,0:T(8,128)S(1)} fusion(f32[32,2560]{1,0:T(8,128)} %fusion.15, bf16[512,2560]{1,0:T(8,128)(2,1)S(1)} %copy-done, f32[48,3072]{1,0:T(8,128)} %reduce_sum.9), kind=kOutput, calls=%fused_computation.17 | convolution fusion | flops 168050688 | bytes 6291456 | tf_op jit(solution)/shard_map/dot_general | solution.py:17
  122.4 6.5 %collective-permute-done.2 = f32[16,2560]{1,0:T(8,128)S(1)} collective-permute-done((f32[16,2560]{1,0:T(8,128)S(1)}, f32[16,2560]{1,0:T(8,128)S(1)}, u32[]{:S(2)}, u32[]{:S(2)}) %collective-permute-start.2) | collective-permute-done | bytes 163872 | tf_op jit(solution)/shard_map/ppermute | solution.py:23
  133.8 3.0 %fusion.5 = f32[16,896]{1,0:T(8,128)S(1)} fusion(bf16[16,2560]{1,0:T(8,128)(2,1)S(1)} %convolution_convert_fusion.1, bf16[1,2560,896]{2,1,0:T(8,128)(2,1)} %param.7), kind=kOutput, calls=%fused_computation.6 | convolution fusion | flops 73400320 | bytes 4726784 | tf_op jit(solution)/shard_map/dot_general | solution.py:17
  139.6 5.4 %collective-permute-done.3 = f32[16,16]{1,0:T(8,128)S(1)} collective-permute-done((f32[16,16]{1,0:T(8,128)S(1)}, f32[16,16]{1,0:T(8,128)S(1)}, u32[]{:S(2)}, u32[]{:S(2)}) %collective-permute-start.3) | collective-permute-done | bytes 1056 | tf_op jit(solution)/shard_map/ppermute | solution.py:23
  145.1 2.0 fusion.16
  147.7 7.1 %collective-permute-done.4 = f32[16,2560]{1,0:T(8,128)S(1)} collective-permute-done((f32[16,2560]{1,0:T(8,128)S(1)}, f32[16,2560]{1,0:T(8,128)S(1)}, u32[]{:S(2)}, u32[]{:S(2)}) %collective-permute-start.4) | collective-permute-done | bytes 163872 | tf_op jit(solution)/shard_map/ppermute | solution.py:23
  156.5 2.1 %cholesky.81 = f32[16,16]{1,0:T(8,128)S(1)} custom-call(f32[16,16]{1,0:T(8,128)} %fusion.63), custom_call_target="Cholesky" | custom-call | tf_op jit(solution)/shard_map/jit(cholesky)/cholesky | solution.py:28
  163.0 3.6 %fusion.3 = f32[16,896]{1,0:T(8,128)} fusion(bf16[16,2560]{1,0:T(8,128)(2,1)S(1)} %convolution_convert_fusion, bf16[1,2560,896]{2,1,0:T(8,128)(2,1)} %param.7), kind=kOutput, calls=%fused_computation.4 | convolution fusion | flops 73400320 | bytes 4726784 | tf_op jit(solution)/shard_map/dot_general | solution.py:17
  166.7 2.5 %fusion.25 = f32[16,896]{1,0:T(8,128)} fusion(f32[16,896]{1,0:T(8,128)} %fusion.3, bf16[512,896]{1,0:T(8,128)(2,1)S(1)} %copy-done.4, bf16[16,2560]{1,0:T(8,128)(2,1)} %copy-done.5, bf16[512,2560]{1,0:T(8,128)(2,1)S(1)} %copy-done), kind=kOutput, calls=%fused_computation.44 | convolution fusion | flops 56659968 | bytes 3735552 | tf_op jit(solution)/shard_map/dot_general | solution.py:17
  169.2 1.8 fusion.24
  171.0 1.9 fusion.23
  172.9 6.1 %fusion.71 = f32[896,2560]{1,0:T(8,128)} fusion(bf16[512,896]{1,0:T(8,128)(2,1)S(1)} %copy-done.4, bf16[512,2560]{1,0:T(8,128)(2,1)S(1)} %copy-done), kind=kOutput, calls=%fused_computation.122 | convolution fusion | flops 2348810240 | bytes 12713984 | tf_op jit(solution)/shard_map/dot_general | solution.py:17
  179.0 7.3 %copy.5 = bf16[1,2560,896]{1,2,0:T(8,128)(2,1)} copy(bf16[1,2560,896]{2,1,0:T(8,128)(2,1)} %param.7) | data formatting | bytes 9175040 | tf_op args[0]
  187.3 7.5 %fusion.2 = bf16[1,2560,896]{1,2,0:T(8,128)(2,1)} fusion(f32[896,2560]{1,0:T(8,128)} %fusion.71, bf16[1,2560,896]{1,2,0:T(8,128)(2,1)} %copy.5, bf16[16,2560]{1,0:T(8,128)(2,1)S(1)} %copy-done.6, bf16[16,2560]{1,0:T(8,128)(2,1)S(1)} %copy-done.10, bf16[16,2560]{1,0:T(8,128)(2,1)S(1)} %copy-done.11, bf16[16,896]{1,0:T(8,128)(2,1)S(1)} %subtract_convert_fusion.2, ...), kind=kOutput, calls=%fused_computation.3 | convolution fusion | flops 234958848 | bytes 18681856 | tf_op jit(solution)/shard_map/dot_general | solution.py:17
  194.8 7.2 %copy.10 = bf16[1,2560,896]{2,1,0:T(8,128)(2,1)} copy(bf16[1,2560,896]{1,2,0:T(8,128)(2,1)} %fusion.2) | data formatting | bytes 9175040 | tf_op jit(solution)/shard_map/broadcast_in_dim | solution.py:66
  (101 shorter events, 34.3 us)
Async XLA Ops:
  6.5 6.3 %copy-start = (bf16[512,2560]{1,0:T(8,128)(2,1)S(1)}, bf16[512,2560]{1,0:T(8,128)(2,1)}, u32[]{:S(2)}) copy-start(bf16[512,2560]{1,0:T(8,128)(2,1)} %param.8) | copy-start | bytes 7864324
  6.5 84.3 %all-gather.3.cloned.1.call-start = ((), (), s32[]{:S(2)}) async-start(), calls=%async_computation | async-start | bytes 5308416 | tf_op jit(solution)/shard_map/all_gather | solution.py:37
  7.6 3.9 %copy-start.8 = (bf16[512,896]{1,0:T(8,128)(2,1)S(1)}, bf16[512,896]{1,0:T(8,128)(2,1)}, u32[]{:S(2)}) copy-start(bf16[512,896]{1,0:T(8,128)(2,1)} %param.9) | copy-start | bytes 2752516
  12.8 1.6 slice-start
  12.8 2.3 %slice-start.1 = ((s8[4587520]{0:T(1024)(128)(4,1)}), s8[4194304]{0:T(1024)(128)(4,1)S(1)}, s32[]{:S(2)}) async-start(s8[4587520]{0:T(1024)(128)(4,1)} %bitcast.109), calls=%async_computation.2 | async-start | bytes 8388608
  12.8 2.5 %copy-start.9 = (bf16[512,896]{1,0:T(8,128)(2,1)S(1)}, bf16[512,896]{1,0:T(8,128)(2,1)}, u32[]{:S(2)}) copy-start(bf16[512,896]{1,0:T(8,128)(2,1)} %param.9) | copy-start | bytes 2752516
  15.4 2.9 %copy-start.12 = (bf16[512,512]{1,0:T(8,128)(2,1)}, bf16[512,512]{1,0:T(8,128)(2,1)S(1)}, u32[]{:S(2)}) copy-start(bf16[512,512]{1,0:T(8,128)(2,1)S(1)} %convolution_convert_fusion.3) | copy-start | bytes 1572868
  97.0 6.9 %collective-permute-start = (f32[16,2560]{1,0:T(8,128)S(1)}, f32[16,2560]{1,0:T(8,128)S(1)}, u32[]{:S(2)}, u32[]{:S(2)}) collective-permute-start(f32[16,2560]{1,0:T(8,128)S(1)} %slice.42), channel_id=1, source_target_pairs={{0,8},{8,16},{16,24},{24,32},{32,40},{40,48},{48,56},{56,64},{64,7... | collective-permute-start | bytes 491528 | tf_op jit(solution)/shard_map/ppermute | solution.py:23
  112.6 5.2 %collective-permute-start.1 = (f32[32,16]{0,1:T(8,128)S(1)}, f32[32,16]{0,1:T(8,128)S(1)}, u32[]{:S(2)}, u32[]{:S(2)}) collective-permute-start(f32[32,16]{0,1:T(8,128)S(1)} %fusion.40), channel_id=1, source_target_pairs={{0,8},{8,16},{16,24},{24,32},{32,40},{40,48},{48,56},{56,64},{64,7... | collective-permute-start | bytes 6152 | tf_op jit(solution)/shard_map/ppermute | solution.py:23
  114.2 7.4 %collective-permute-start.5 = (f32[16,896]{1,0:T(8,128)}, f32[16,896]{1,0:T(8,128)}, u32[]{:S(2)}, u32[]{:S(2)}) collective-permute-start(f32[16,896]{1,0:T(8,128)} %fusion.28), channel_id=1, source_target_pairs={{0,8},{8,16},{16,24},{24,32},{32,40},{40,48},{48,56},{56,64},{64,7... | collective-permute-start | bytes 172040 | tf_op jit(solution)/shard_map/ppermute | solution.py:23
  121.3 7.7 %collective-permute-start.2 = (f32[16,2560]{1,0:T(8,128)S(1)}, f32[16,2560]{1,0:T(8,128)S(1)}, u32[]{:S(2)}, u32[]{:S(2)}) collective-permute-start(f32[16,2560]{1,0:T(8,128)S(1)} %slice.45), channel_id=1, source_target_pairs={{0,16},{8,24},{16,32},{24,40},{32,48},{40,56},{48,64},{56,72},{64,... | collective-permute-start | bytes 491528 | tf_op jit(solution)/shard_map/ppermute | solution.py:23
  122.4 16.7 %copy-start.13 = (bf16[16,896]{1,0:T(8,128)(2,1)}, bf16[16,896]{1,0:T(8,128)(2,1)S(1)}, u32[]{:S(2)}) copy-start(bf16[16,896]{1,0:T(8,128)(2,1)S(1)} %subtract_convert_fusion.4) | copy-start | bytes 86020
  136.8 2.1 copy-start.1
  139.1 5.8 %collective-permute-start.3 = (f32[16,16]{1,0:T(8,128)S(1)}, f32[16,16]{1,0:T(8,128)S(1)}, u32[]{:S(2)}, u32[]{:S(2)}) collective-permute-start(f32[16,16]{1,0:T(8,128)S(1)} %fusion.54), channel_id=1, source_target_pairs={{0,16},{8,24},{16,32},{24,40},{32,48},{40,56},{48,64},{56,72},{64,... | collective-permute-start | bytes 3080 | tf_op jit(solution)/shard_map/ppermute | solution.py:23
  139.5 7.6 %collective-permute-start.6 = (f32[16,896]{1,0:T(8,128)S(1)}, f32[16,896]{1,0:T(8,128)S(1)}, u32[]{:S(2)}, u32[]{:S(2)}) collective-permute-start(f32[16,896]{1,0:T(8,128)S(1)} %fusion.26), channel_id=1, source_target_pairs={{0,16},{8,24},{16,32},{24,40},{32,48},{40,56},{48,64},{56,72},{64,... | collective-permute-start | bytes 172040 | tf_op jit(solution)/shard_map/ppermute | solution.py:23
  147.0 7.7 %collective-permute-start.4 = (f32[16,2560]{1,0:T(8,128)S(1)}, f32[16,2560]{1,0:T(8,128)S(1)}, u32[]{:S(2)}, u32[]{:S(2)}) collective-permute-start(f32[16,2560]{1,0:T(8,128)S(1)} %fusion.16), channel_id=1, source_target_pairs={{0,32},{8,40},{16,48},{24,56},{32,64},{40,72},{48,80},{56,88},{64,... | collective-permute-start | bytes 491528 | tf_op jit(solution)/shard_map/ppermute | solution.py:23
  155.5 11.2 %copy-start.4 = (bf16[512,896]{1,0:T(8,128)(2,1)S(1)}, bf16[512,896]{1,0:T(8,128)(2,1)}, u32[]{:S(2)}) copy-start(bf16[512,896]{1,0:T(8,128)(2,1)} %subtract_convert_fusion) | copy-start | bytes 2752516
  172.9 13.5 %collective-permute-start.7 = (f32[16,896]{1,0:T(8,128)}, f32[16,896]{1,0:T(8,128)}, u32[]{:S(2)}, u32[]{:S(2)}) collective-permute-start(f32[16,896]{1,0:T(8,128)} %fusion.23), channel_id=1, source_target_pairs={{0,32},{8,40},{16,48},{24,56},{32,64},{40,72},{48,80},{56,88},{64,... | collective-permute-start | bytes 172040 | tf_op jit(solution)/shard_map/ppermute | solution.py:23
  179.0 7.4 %copy-start.16 = (f32[16,896]{1,0:T(8,128)S(1)}, f32[16,896]{1,0:T(8,128)}, u32[]{:S(2)}) copy-start(f32[16,896]{1,0:T(8,128)} %fusion.23) | copy-start | bytes 172036
  179.0 8.2 %copy-start.6 = (bf16[16,2560]{1,0:T(8,128)(2,1)S(1)}, bf16[16,2560]{1,0:T(8,128)(2,1)}, u32[]{:S(2)}) copy-start(bf16[16,2560]{1,0:T(8,128)(2,1)} %copy-done.5) | copy-start | bytes 245764
  179.0 8.2 %copy-start.10 = (bf16[16,2560]{1,0:T(8,128)(2,1)S(1)}, bf16[16,2560]{1,0:T(8,128)(2,1)}, u32[]{:S(2)}) copy-start(bf16[16,2560]{1,0:T(8,128)(2,1)} %subtract_convert_fusion.1) | copy-start | bytes 245764
  179.0 8.2 %copy-start.11 = (bf16[16,2560]{1,0:T(8,128)(2,1)S(1)}, bf16[16,2560]{1,0:T(8,128)(2,1)}, u32[]{:S(2)}) copy-start(bf16[16,2560]{1,0:T(8,128)(2,1)} %fusion.19) | copy-start | bytes 245764
  179.0 8.2 %copy-start.14 = (bf16[16,896]{1,0:T(8,128)(2,1)S(1)}, bf16[16,896]{1,0:T(8,128)(2,1)}, u32[]{:S(2)}) copy-start(bf16[16,896]{1,0:T(8,128)(2,1)} %copy-done.13) | copy-start | bytes 86020
  179.0 8.2 %copy-start.15 = (bf16[16,896]{1,0:T(8,128)(2,1)S(1)}, bf16[16,896]{1,0:T(8,128)(2,1)}, u32[]{:S(2)}) copy-start(bf16[16,896]{1,0:T(8,128)(2,1)} %subtract_convert_fusion.3) | copy-start | bytes 86020
  (4 other events, 4.1 us)
Sparse Core Ops, SparseCore 0:
  12.9 77.8 all-gather.2
